TPU v7x, 512 devices: a whole 4x8x8 slice. The times are simulated.
512 devices in a mesh: space: 32 (over z_hi, x, core), chan: 16 (over z_lo, y).
Axes of the slice: x: 4, y: 8, z: 8 (z_hi: 4, z_lo: 2; z = z_hi * 2 + z_lo), core: 2. Of those that a mesh axis runs over, the one named last changes fastest.
Arguments:
- volume: bfloat16 [128, 128, 16, 128], P('chan', 'space'), may hold values from -6 to 6
- kernel: bfloat16 [128, 3, 3, 3, 128], P('chan'), may hold values from -0.109375 to 0.109375
- upstream: bfloat16 [128, 32, 4, 32], P('chan', 'space'), may hold values from -24 to 24
Outputs:
- pooled: bfloat16 [128, 32, 4, 32], P('chan', 'space')
- volume_grad: bfloat16 [128, 128, 16, 128], P('chan', 'space')
- kernel_grad: float32 [128, 3, 3, 3, 128], P('chan')
All inputs are finite; a program needn't handle non-finite values.
Results may differ from a plain program's by a relative error of at most 0.013.
Values may be sent and summed in bfloat16 or wider, within the bound.
A program may use at most 64 MiB of HBM per device.

v0:
```python
import jax
import jax.numpy as jnp
from jax import lax
from jax.sharding import PartitionSpec as P

slope_neg = 0.3
tap_table = ((1, 0, 0), (2, 1, 0), (0, 1, 1))


def from_behind(block, axis, distance):
    devices = range(lax.axis_size(axis))
    route = [(i - distance, i) for i in devices if i - distance in devices]
    return lax.ppermute(block, axis, route)


def strided_conv(operand, filters):
    return lax.conv_general_dilated(
        operand[None],
        filters,
        (2, 2, 2),
        ((0, 0), (1, 1), (1, 1)),
        dimension_numbers=("NCDHW", "IDHWO", "NCDHW"),
        preferred_element_type=jnp.float32,
    )[0]


def on_device(volume, kernel, upstream):
    in_block = volume.shape[0]
    out_block = upstream.shape[0]
    out_depth = volume.shape[1] // 2
    out_rows = volume.shape[2] // 2
    out_cols = volume.shape[3] // 2
    lower_rim = from_behind(volume[:, -1:], "space", 1)
    padded = jnp.concatenate([lower_rim, volume], axis=1)
    own_first = lax.axis_index("chan") * out_block
    empty = jnp.zeros((out_block, out_depth, out_rows, out_cols), jnp.float32)
    columns = lax.dynamic_slice_in_dim(
        lax.all_gather(kernel, "chan", axis=0, tiled=True), own_first, out_block, 4
    )
    pre = empty + strided_conv(lax.all_gather(padded, "chan", axis=0, tiled=True), columns)
    activated = jnp.where(pre > 0, pre, slope_neg * pre)
    block_shape = (out_block, out_depth // 2, 2, out_rows // 2, 2, out_cols // 2, 2)
    pooled = jnp.mean(activated.reshape(block_shape), axis=(2, 4, 6)).astype(jnp.bfloat16)
    spread = upstream.astype(jnp.float32) * 0.125
    spread = jnp.broadcast_to(spread[:, :, None, :, None, :, None], block_shape).reshape(pre.shape)
    pre_grad = (spread * jnp.where(pre > 0, 1.0, slope_neg)).astype(jnp.bfloat16)
    upper_rim = from_behind(pre_grad[:, :1], "space", -1)
    extended = jnp.concatenate([pre_grad, upper_rim], axis=1)
    panel = lax.all_gather(extended, "chan", axis=0, tiled=True)
    offset = jnp.int32(0)
    phase_grad = jnp.zeros((2, 2, 2, in_block, out_depth, out_rows, out_cols), jnp.float32)
    weight_grad = jnp.zeros((in_block, 3, 3, 3, kernel.shape[4]), jnp.float32)
    columns = lax.dynamic_slice_in_dim(kernel, offset, panel.shape[0], 4)
    grad_pad = jnp.pad(panel, ((0, 0), (0, 0), (0, 1), (0, 1)))
    phase_sums = {}
    for depth_tap, depth_par, depth_off in tap_table:
        for row_tap, row_par, row_off in tap_table:
            for col_tap, col_par, col_off in tap_table:
                shifted = grad_pad[
                    :,
                    depth_off : depth_off + out_depth,
                    row_off : row_off + out_rows,
                    col_off : col_off + out_cols,
                ]
                term = jnp.einsum(
                    "co,ozyx->czyx",
                    columns[:, depth_tap, row_tap, col_tap, :],
                    shifted,
                    preferred_element_type=jnp.float32,
                )
                phase_key = (depth_par, row_par, col_par)
                if phase_key in phase_sums:
                    phase_sums[phase_key] = phase_sums[phase_key] + term
                else:
                    phase_sums[phase_key] = term
    stacked = jnp.stack(
        [
            phase_sums[first, second, third]
            for first in (0, 1)
            for second in (0, 1)
            for third in (0, 1)
        ]
    )
    phase_grad = stacked.reshape(phase_grad.shape)
    weight_part = lax.conv_general_dilated(
        padded[None],
        panel[:, :out_depth][None],
        (1, 1, 1),
        ((0, 0), (1, 0), (1, 0)),
        rhs_dilation=(2, 2, 2),
        dimension_numbers=("CNDHW", "IODHW", "NDHWC"),
        preferred_element_type=jnp.float32,
    )
    weight_grad = lax.dynamic_update_slice_in_dim(weight_grad, weight_part, offset, 4)
    phase_grad, weight_grad = (phase_grad, weight_grad)
    input_grad = phase_grad.transpose(3, 4, 0, 5, 1, 6, 2).reshape(volume.shape)
    kernel_grad = lax.psum(weight_grad, "space")
    return (pooled, input_grad.astype(jnp.bfloat16), kernel_grad)


def solution(mesh):
    return jax.shard_map(
        on_device,
        mesh=mesh,
        in_specs=(
            P("chan", "space", None, None),
            P("chan", None, None, None, None),
            P("chan", "space", None, None),
        ),
        out_specs=(
            P("chan", "space", None, None),
            P("chan", "space", None, None),
            P("chan", None, None, None, None),
        ),
        check_vma=False,
    )
```

profile of v0, /device:TPU:1, one launch (start us, length us, event | category | flops | bytes accessed | tf_op | source)
XLA Modules:
  0.0 439.3 jit_solution(8369169473924084968)
XLA Ops:
  7.2 0.8 slice.133
  8.0 4.5 %collective-permute-start = (bf16[8,1,16,128]{3,2,1,0:T(8,128)(2,1)S(1)}, bf16[8,1,16,128]{3,2,1,0:T(8,128)(2,1)S(1)}, u32[]{:S(2)}, u32[]{:S(2)}) collective-permute-start(bf16[8,1,16,128]{3,2,1,0:T(8,128)(2,1)S(1)} %slice.133), channel_id=1, source_target_pairs={{0,16},{16,32},{32,48},{48,64},{64,80},{80,96},{96,112},{112,128},... | collective-permute-start | bytes 98312 | tf_op jit(solution)/shard_map/ppermute | solution.py:13
  12.5 4.3 collective-permute-done
  16.8 0.9 constant_dynamic-update-slice_fusion
  17.7 0.7 copy-done
  18.5 0.7 multiply_bitcast_fusion
  19.4 33.0 %all_gather.10 = bf16[128,3,3,3,128]{4,0,3,2,1:T(8,128)(2,1)S(1)} all-gather(bf16[8,3,3,3,128]{4,0,3,2,1:T(8,128)(2,1)} %param.4), channel_id=1, replica_groups=mesh['space'=32,'chan'=16] {'chan'}, dimensions={0}, use_global_device_ids=true | all-gather | bytes 940032 | tf_op jit(solution)/shard_map/all_gather | solution.py:38
  52.5 7.8 %copy.75 = bf16[1,8,5,16,128]{1,0,4,3,2:T(2,128)(2,1)} copy(bf16[1,8,5,16,128]{4,3,2,1,0:T(8,128)(2,1)} %bitcast.294) | data formatting | bytes 327680 | tf_op jit(solution)/shard_map/broadcast_in_dim | solution.py:86
  60.3 27.8 %all-gather.2.cloned.1.call-done = bf16[128,5,16,128]{3,2,1,0:T(8,128)(2,1)} async-done(((bf16[8,5,16,128]{3,2,1,0:T(8,128)(2,1)}), bf16[128,5,16,128]{3,2,1,0:T(8,128)(2,1)}) %all-gather.2.cloned.1.call-update) | async-done | bytes 2621456 | tf_op jit(solution)/shard_map/all_gather | solution.py:40
  88.1 4.6 %copy.60 = bf16[128,5,16,128]{0,2,3,1:T(8,128)(2,1)S(1)} copy(bf16[128,5,16,128]{3,2,1,0:T(8,128)(2,1)} %all-gather.2.cloned.1.call-done) | data formatting | bytes 5242880 | tf_op jit(solution)/shard_map/all_gather | solution.py:40
  92.8 0.5 pad.5
  93.3 1.1 copy.62
  94.5 2.3 compare_select_fusion
  96.9 0.8 copy.68
  97.9 11.7 %collective-permute-start.1 = (bf16[8,1,8,64]{3,0,2,1:T(8,128)(2,1)S(1)}, bf16[8,1,8,64]{3,0,2,1:T(8,128)(2,1)S(1)}, u32[]{:S(2)}, u32[]{:S(2)}) collective-permute-start(bf16[8,1,8,64]{3,0,2,1:T(8,128)(2,1)S(1)} %slice.176), channel_id=1, source_target_pairs={{16,0},{32,16},{48,32},{64,48},{80,64},{96,80},{112,96},{128,112},... | collective-permute-start | bytes 24584 | tf_op jit(solution)/shard_map/ppermute | solution.py:13
  109.6 0.8 copy.64
  111.0 0.7 copy.77
  111.7 1.1 collective-permute-done.1
  112.9 30.1 %all_gather.11 = bf16[128,3,8,64]{3,2,1,0:T(8,128)(2,1)S(1)} all-gather(bf16[8,3,8,64]{3,2,1,0:T(8,128)(2,1)S(1)} %pad_maximum_fusion), channel_id=1, replica_groups=mesh['space'=32,'chan'=16] {'chan'}, dimensions={0}, use_global_device_ids=true | all-gather | bytes 417792 | tf_op jit(solution)/shard_map/all_gather | solution.py:49
  143.0 0.5 copy.71
  144.3 0.3 fusion.83
  144.6 0.3 fusion.74
  145.0 0.3 fusion.64
  145.3 0.3 fusion.52
  145.6 0.3 fusion.50
  145.9 0.3 fusion.48
  146.5 0.3 fusion.49
  146.8 0.3 fusion.51
  147.1 0.3 fusion.53
  147.4 0.3 fusion.47
  147.7 0.3 fusion.78
  148.0 0.3 fusion.89
  148.3 0.3 fusion.29
  148.6 0.3 convolution_add_fusion.3
  148.9 0.3 convolution_add_fusion.5
  149.3 13.7 %fusion.45 = f32[8,3,3,3,128]{4,0,3,2,1:T(8,128)} fusion(bf16[1,8,5,16,128]{1,0,4,3,2:T(2,128)(2,1)} %copy.75, bf16[1,128,2,8,64]{1,4,3,2,0:T(8,128)(2,1)S(1)} %slice_bitcast_fusion), kind=kOutput, calls=%fused_computation.56 | convolution fusion | flops 53981184 | bytes 536576 | tf_op jit(solution)/shard_map/conv_general_dilated | solution.py:85
  162.9 0.3 fusion.41
  163.2 0.3 fusion.39
  163.6 0.3 fusion.37
  163.9 0.3 fusion.35
  164.2 0.3 fusion.15
  164.6 0.3 fusion.33
  164.9 0.3 fusion.31
  165.2 0.3 fusion.43
  165.6 1.5 copy.74
  167.0 1.5 copy.78
  168.5 262.4 %all-reduce.3.cloned.1.call-done = f32[8,3,3,3,128]{4,0,3,2,1:T(8,128)} async-done(((f32[8,3,3,3,128]{4,0,3,2,1:T(8,128)}), f32[8,3,3,3,128]{4,0,3,2,1:T(8,128)}) %all-reduce.3.cloned.1.call-update) | async-done | bytes 110608 | tf_op jit(solution)/shard_map/psum | solution.py:97
  430.9 1.5 copy.118
  (30 shorter events, 2.4 us)
Async XLA Ops:
  7.2 81.0 %all-gather.2.cloned.1.call-start = ((), (), s32[]{:S(2)}) async-start(), calls=%async_computation | async-start | bytes 2785280 | tf_op jit(solution)/shard_map/all_gather | solution.py:40
  8.0 8.8 %collective-permute-start = (bf16[8,1,16,128]{3,2,1,0:T(8,128)(2,1)S(1)}, bf16[8,1,16,128]{3,2,1,0:T(8,128)(2,1)S(1)}, u32[]{:S(2)}, u32[]{:S(2)}) collective-permute-start(bf16[8,1,16,128]{3,2,1,0:T(8,128)(2,1)S(1)} %slice.133), channel_id=1, source_target_pairs={{0,16},{16,32},{32,48},{48,64},{64,80},{80,96},{96,112},{112,128},... | collective-permute-start | bytes 98312 | tf_op jit(solution)/shard_map/ppermute | solution.py:13
  17.7 0.7 copy-start
  18.4 412.5 %all-reduce.3.cloned.1.call-start = ((), (), s32[]{:S(2)}) async-start(), calls=%async_computation.1 | async-start | bytes 221184 | tf_op jit(solution)/shard_map/psum | solution.py:97
  93.3 1.3 copy-start.2
  96.8 46.6 %copy-start.1 = (bf16[8,3,3,3,128]{4,0,3,2,1:T(8,128)(2,1)S(1)}, bf16[8,3,3,3,128]{4,0,3,2,1:T(8,128)(2,1)}, u32[]{:S(2)}) copy-start(bf16[8,3,3,3,128]{4,0,3,2,1:T(8,128)(2,1)} %param.4) | copy-start | bytes 165892
  97.9 15.0 %collective-permute-start.1 = (bf16[8,1,8,64]{3,0,2,1:T(8,128)(2,1)S(1)}, bf16[8,1,8,64]{3,0,2,1:T(8,128)(2,1)S(1)}, u32[]{:S(2)}, u32[]{:S(2)}) collective-permute-start(bf16[8,1,8,64]{3,0,2,1:T(8,128)(2,1)S(1)} %slice.176), channel_id=1, source_target_pairs={{16,0},{32,16},{48,32},{64,48},{80,64},{96,80},{112,96},{128,112},... | collective-permute-start | bytes 24584 | tf_op jit(solution)/shard_map/ppermute | solution.py:13
Sparse Core Ops, SparseCore 0:
  18.5 69.5 all-gather.1
  163.1 267.7 all-reduce.2
where the time goes:
time: 440 us; the launch traced here: 439 us
  waiting for transfers between devices  296 us (67%)
  blocking collectives  63.1 us (14%)
  local copies, waits for them, and re-layouts  24.7 us (6%)
  matrix products  24.3 us (6%)
  starting transfers between devices  16.3 us (4%)
  between operations  14.3 us (3%)
    psum x1, waiting for transfers between devices, on_device(): kernel_grad = lax.psum(weight_grad, 'space')  262 us
    all_gather x1, blocking collectives, on_device(): lax.all_gather(kernel, 'chan', axis=0, tiled=True)  33 us
    all_gather x1, blocking collectives, on_device(): panel = lax.all_gather(extended, 'chan', axis=0, tiled=True)  30.1 us
    all_gather x1, waiting for transfers between devices, on_device(): lax.all_gather(padded, 'chan', axis=0, tiled=True)  27.8 us
    ppermute x2, starting transfers between devices, from_behind(): return lax.ppermute(block, axis, route)  16.2 us
    conv_general_dilated x1, matrix products, on_device(): lax.conv_general_dilated(padded[None], panel[:, :out_depth][None], (1, 1,...  13.7 us
  transfers between devices with their start and end apart: 4, of which 4 were waited for; matrix products, arithmetic and copies ran while one was open for 4% of the time, Pallas kernels for 0%

commit v1 on v0

--- a/solution.py
+++ b/solution.py
@@ -94,7 +94,7 @@
     weight_grad = lax.dynamic_update_slice_in_dim(weight_grad, weight_part, offset, 4)
     phase_grad, weight_grad = (phase_grad, weight_grad)
     input_grad = phase_grad.transpose(3, 4, 0, 5, 1, 6, 2).reshape(volume.shape)
-    kernel_grad = lax.psum(weight_grad, "space")
+    kernel_grad = jnp.sum(lax.all_gather(weight_grad, "space"), axis=0)
     return (pooled, input_grad.astype(jnp.bfloat16), kernel_grad)
 
 

time: 440 us -> 240 us (0.55)
  waiting for transfers between devices: 296 us -> 96.2 us
    psum x1 -> x0, waiting for transfers between devices: 262 us -> none  [on_device(): kernel_grad = lax.psum(weight_grad, 'space')]
    all_gather x0 -> x1, waiting for transfers between devices: none -> 56.2 us  [on_device(): kernel_grad = jnp.sum(lax.all_gather(weight_grad, 'space'), axis=0)]
    all_gather x1, waiting for transfers between devices: 27.8 us -> 35.7 us  [on_device(): lax.all_gather(padded, 'chan', axis=0, tiled=True)]
  transfers between devices with their start and end apart: 4 -> 4, of which waited for: 4 -> 3; matrix products, arithmetic and copies ran while one was open for 4% -> 8% of each run, Pallas kernels for 0% -> 0%
where the time goes in v1:
time: 240 us
  waiting for transfers between devices  96.2 us (40%)
  blocking collectives  64 us (27%)
  matrix products  24.3 us (10%)
  local copies, waits for them, and re-layouts  21 us (9%)
  starting transfers between devices  16.3 us (7%)
  between operations  14.3 us (6%)
  other arithmetic  3.81 us (2%)
    all_gather x1, waiting for transfers between devices, on_device(): kernel_grad = jnp.sum(lax.all_gather(weight_grad, 'space'), axis=0)  56.2 us
    all_gather x1, waiting for transfers between devices, on_device(): lax.all_gather(padded, 'chan', axis=0, tiled=True)  35.7 us
    all_gather x1, blocking collectives, on_device(): lax.all_gather(kernel, 'chan', axis=0, tiled=True)  33 us
    all_gather x1, blocking collectives, on_device(): panel = lax.all_gather(extended, 'chan', axis=0, tiled=True)  31 us
    ppermute x2, starting transfers between devices, from_behind(): return lax.ppermute(block, axis, route)  16.2 us
    conv_general_dilated x1, matrix products, on_device(): lax.conv_general_dilated(padded[None], panel[:, :out_depth][None], (1, 1,...  13.6 us
    dot_general x27, matrix products, on_device(): jnp.einsum('co,ozyx->czyx', columns[:, depth_tap, row_tap, col_tap, :], s...  8.36 us
    broadcast_in_dim x1, local copies, waits for them, and re-layouts, on_device(): padded[None]  5.69 us
  transfers between devices with their start and end apart: 4, of which 3 were waited for; matrix products, arithmetic and copies ran while one was open for 8% of the time, Pallas kernels for 0%

profile of v1, /device:TPU:1, one launch (start us, length us, event | category | flops | bytes accessed | tf_op | source)
XLA Modules:
  0.0 239.9 jit_solution(8670026480079002578)
XLA Ops:
  7.2 0.8 slice.133
  8.0 4.5 %collective-permute-start = (bf16[8,1,16,128]{3,2,1,0:T(8,128)(2,1)S(1)}, bf16[8,1,16,128]{3,2,1,0:T(8,128)(2,1)S(1)}, u32[]{:S(2)}, u32[]{:S(2)}) collective-permute-start(bf16[8,1,16,128]{3,2,1,0:T(8,128)(2,1)S(1)} %slice.133), channel_id=1, source_target_pairs={{0,16},{16,32},{32,48},{48,64},{64,80},{80,96},{96,112},{112,128},... | collective-permute-start | bytes 98312 | tf_op jit(solution)/shard_map/ppermute | solution.py:13
  12.5 4.3 %collective-permute-done = bf16[8,1,16,128]{3,2,1,0:T(8,128)(2,1)S(1)} collective-permute-done((bf16[8,1,16,128]{3,2,1,0:T(8,128)(2,1)S(1)}, bf16[8,1,16,128]{3,2,1,0:T(8,128)(2,1)S(1)}, u32[]{:S(2)}, u32[]{:S(2)}) %collective-permute-start) | collective-permute-done | bytes 32800 | tf_op jit(solution)/shard_map/ppermute | solution.py:13
  16.8 0.9 constant_dynamic-update-slice_fusion
  17.7 0.7 copy-done
  18.5 0.7 multiply_bitcast_fusion
  19.4 33.0 %all_gather.16 = bf16[128,3,3,3,128]{4,0,3,2,1:T(8,128)(2,1)S(1)} all-gather(bf16[8,3,3,3,128]{4,0,3,2,1:T(8,128)(2,1)} %param.4), channel_id=1, replica_groups=mesh['space'=32,'chan'=16] {'chan'}, dimensions={0}, use_global_device_ids=true | all-gather | bytes 940032 | tf_op jit(solution)/shard_map/all_gather | solution.py:38
  52.5 35.7 %all-gather.4.cloned.1.call-done = bf16[128,5,16,128]{3,2,1,0:T(8,128)(2,1)} async-done(((bf16[8,5,16,128]{3,2,1,0:T(8,128)(2,1)}), bf16[128,5,16,128]{3,2,1,0:T(8,128)(2,1)}) %all-gather.4.cloned.1.call-update) | async-done | bytes 2621456 | tf_op jit(solution)/shard_map/all_gather | solution.py:40
  88.1 4.6 %copy.60 = bf16[128,5,16,128]{0,2,3,1:T(8,128)(2,1)S(1)} copy(bf16[128,5,16,128]{3,2,1,0:T(8,128)(2,1)} %all-gather.4.cloned.1.call-done) | data formatting | bytes 5242880 | tf_op jit(solution)/shard_map/all_gather | solution.py:40
  92.8 0.5 pad.5
  93.3 1.1 copy.62
  94.5 2.3 compare_select_fusion
  96.9 0.8 copy.68
  97.9 11.7 %collective-permute-start.1 = (bf16[8,1,8,64]{3,0,2,1:T(8,128)(2,1)S(1)}, bf16[8,1,8,64]{3,0,2,1:T(8,128)(2,1)S(1)}, u32[]{:S(2)}, u32[]{:S(2)}) collective-permute-start(bf16[8,1,8,64]{3,0,2,1:T(8,128)(2,1)S(1)} %slice.176), channel_id=1, source_target_pairs={{16,0},{32,16},{48,32},{64,48},{80,64},{96,80},{112,96},{128,112},... | collective-permute-start | bytes 24584 | tf_op jit(solution)/shard_map/ppermute | solution.py:13
  109.6 5.7 %copy.75 = bf16[1,8,5,16,128]{1,0,4,3,2:T(2,128)(2,1)} copy(bf16[1,8,5,16,128]{4,3,2,1,0:T(8,128)(2,1)S(1)} %bitcast.296) | data formatting | bytes 327680 | tf_op jit(solution)/shard_map/broadcast_in_dim | solution.py:86
  115.4 31.0 %all_gather.17 = bf16[128,3,8,64]{3,2,1,0:T(8,128)(2,1)S(1)} all-gather(bf16[8,3,8,64]{3,2,1,0:T(8,128)(2,1)S(1)} %pad_maximum_fusion), channel_id=1, replica_groups=mesh['space'=32,'chan'=16] {'chan'}, dimensions={0}, use_global_device_ids=true | all-gather | bytes 417792 | tf_op jit(solution)/shard_map/all_gather | solution.py:49
  146.4 0.5 copy.71
  146.9 13.6 %fusion.45 = f32[8,3,3,3,128]{4,0,3,2,1:T(8,128)} fusion(bf16[1,8,5,16,128]{1,0,4,3,2:T(2,128)(2,1)} %copy.75, bf16[1,128,2,8,64]{1,4,3,2,0:T(8,128)(2,1)S(1)} %slice_bitcast_fusion), kind=kOutput, calls=%fused_computation.57 | convolution fusion | flops 53981184 | bytes 536576 | tf_op jit(solution)/shard_map/conv_general_dilated | solution.py:85
  160.6 0.8 copy.64
  162.0 0.7 copy.77
  163.0 0.3 fusion.69
  163.5 0.3 fusion.83
  163.8 0.3 fusion.74
  164.2 0.3 fusion.64
  164.5 0.3 fusion.52
  164.8 0.3 fusion.50
  165.1 0.3 fusion.48
  165.7 0.3 fusion.49
  165.9 0.3 fusion.51
  166.3 0.3 fusion.53
  166.6 0.3 fusion.47
  166.8 0.3 fusion.89
  167.2 0.3 fusion.29
  167.5 0.3 fusion.78
  167.8 0.3 fusion.41
  168.1 0.3 fusion.39
  168.4 0.3 fusion.37
  168.8 0.3 fusion.35
  169.1 0.3 convolution_add_fusion.3
  169.4 0.3 convolution_add_fusion.5
  169.7 0.3 fusion.33
  170.1 0.3 fusion.31
  170.4 0.3 fusion.15
  170.7 0.3 fusion.43
  171.1 1.5 copy.74
  172.6 1.5 copy.78
  174.0 56.2 %all-gather.6.cloned.1.call-done = f32[256,3,3,3,128]{4,0,3,2,1:T(8,128)} async-done(((f32[8,3,3,3,128]{4,0,3,2,1:T(8,128)}), f32[256,3,3,3,128]{4,0,3,2,1:T(8,128)}) %all-gather.6.cloned.1.call-update) | async-done | bytes 3538960 | tf_op jit(solution)/shard_map/all_gather | solution.py:97
  230.3 2.9 %bitcast_reduce_fusion = f32[8,3,3,3,128]{4,0,3,2,1:T(8,128)} fusion(f32[256,3,3,3,128]{4,0,3,2,1:T(8,128)} %all-gather.6.cloned.1.call-done), kind=kLoop, calls=%fused_computation.2 | loop fusion | flops 857088 | bytes 3649536 | tf_op jit(solution)/shard_map/reduce_sum | solution.py:97
  (32 shorter events, 2.1 us)
Async XLA Ops:
  7.2 81.0 %all-gather.4.cloned.1.call-start = ((), (), s32[]{:S(2)}) async-start(), calls=%async_computation | async-start | bytes 2785280 | tf_op jit(solution)/shard_map/all_gather | solution.py:40
  8.0 8.8 %collective-permute-start = (bf16[8,1,16,128]{3,2,1,0:T(8,128)(2,1)S(1)}, bf16[8,1,16,128]{3,2,1,0:T(8,128)(2,1)S(1)}, u32[]{:S(2)}, u32[]{:S(2)}) collective-permute-start(bf16[8,1,16,128]{3,2,1,0:T(8,128)(2,1)S(1)} %slice.133), channel_id=1, source_target_pairs={{0,16},{16,32},{32,48},{48,64},{64,80},{80,96},{96,112},{112,128},... | collective-permute-start | bytes 98312 | tf_op jit(solution)/shard_map/ppermute | solution.py:13
  17.7 0.7 copy-start
  18.4 211.8 %all-gather.6.cloned.1.call-start = ((), (), s32[]{:S(2)}) async-start(), calls=%async_computation.1 | async-start | bytes 3649536 | tf_op jit(solution)/shard_map/all_gather | solution.py:97
  93.3 1.3 copy-start.3
  94.5 15.1 %copy-start.1 = (bf16[8,5,16,128]{3,2,1,0:T(8,128)(2,1)S(1)}, bf16[8,5,16,128]{3,2,1,0:T(8,128)(2,1)}, u32[]{:S(2)}) copy-start(bf16[8,5,16,128]{3,2,1,0:T(8,128)(2,1)} %copy-done) | copy-start | bytes 491524
  97.9 17.4 %collective-permute-start.1 = (bf16[8,1,8,64]{3,0,2,1:T(8,128)(2,1)S(1)}, bf16[8,1,8,64]{3,0,2,1:T(8,128)(2,1)S(1)}, u32[]{:S(2)}, u32[]{:S(2)}) collective-permute-start(bf16[8,1,8,64]{3,0,2,1:T(8,128)(2,1)S(1)} %slice.176), channel_id=1, source_target_pairs={{16,0},{32,16},{48,32},{64,48},{80,64},{96,80},{112,96},{128,112},... | collective-permute-start | bytes 24584 | tf_op jit(solution)/shard_map/ppermute | solution.py:13
  146.9 15.8 %copy-start.2 = (bf16[8,3,3,3,128]{4,0,3,2,1:T(8,128)(2,1)S(1)}, bf16[8,3,3,3,128]{4,0,3,2,1:T(8,128)(2,1)}, u32[]{:S(2)}) copy-start(bf16[8,3,3,3,128]{4,0,3,2,1:T(8,128)(2,1)} %param.4) | copy-start | bytes 165892
Sparse Core Ops, SparseCore 0:
  18.5 69.5 all-gather.3
  160.7 69.4 all-gather.5
